TPU v7x, 128 devices: a whole 4x4x4 slice. The times are simulated.
128 devices in a mesh: dp: 8 (over z, core), vocab: 16 (over y, x).
Axes of the slice: x: 4, y: 4, z: 4, core: 2. Of those that a mesh axis runs over, the one named last changes fastest.
Arguments:
- hidden: bfloat16 [12288, 896], P(('dp', 'vocab')), may hold values from -400 to 400
- target_ids: int32 [12288], P('dp'), may hold values from 0 to 151935
- owner: int32 [8, 48], P('dp'), may hold values from 0 to 47, each once within a row
- head: bfloat16 [896, 151936], P(None, 'vocab'), may hold values from -0.1875 to 0.1875
Outputs:
- owned_loss: float32 [384, 32], P(('dp', 'vocab'))
Inputs may be any that keep to these rules, and one draw needn't show every extreme that they name: Each row of owner names every slot once.
All inputs are finite; a program needn't handle non-finite values.
Results may differ from a plain program's by a relative error of at most 0.0003.
Values may be sent and summed in bfloat16 or wider, within the bound.
A program may use at most 128 MiB of HBM per device.

v0:
```python
import math

import jax
import jax.numpy as jnp
from jax import lax
from jax.sharding import PartitionSpec as P


def side_by_side(arrays, axis, split_dim, concat_dim, along):
    ends, at = ([], 0)
    for a in arrays[:-1]:
        at += a.shape[along]
        ends.append(at)
    both = jnp.concatenate(arrays, axis=along)
    return tuple(
        jnp.split(
            lax.all_to_all(both, axis, split_axis=split_dim, concat_axis=concat_dim, tiled=True),
            ends,
            axis=along,
        )
    )


def local(hidden, target_ids, owner, head):
    width = head.shape[1]
    base = lax.axis_index("vocab") * width

    def partials(rows, labels):
        logits = jnp.dot(rows, head, preferred_element_type=jnp.float32)
        peak = jnp.max(logits, axis=1)
        expsum = jnp.sum(jnp.exp(logits - peak[:, None]), axis=1)
        column = lax.broadcasted_iota(jnp.int32, logits.shape, 1)
        picked = jnp.sum(jnp.where(column == (labels - base)[:, None], logits, 0.0), axis=1)
        return jnp.stack((peak, expsum, picked), 0)

    gathered = lax.all_gather(hidden, "vocab", axis=0, tiled=True)
    count = gathered.shape[0]
    step_rows = math.gcd(count, 512)
    split_rows = gathered.reshape(count // step_rows, step_rows, gathered.shape[1])
    split_labels = target_ids.reshape(count // step_rows, step_rows)
    results = lax.map(lambda pair: partials(pair[0], pair[1]), (split_rows, split_labels))
    stats = jnp.transpose(results, (1, 0, 2)).reshape(3, count)
    peak, expsum, picked = (stats[0], stats[1], stats[2])
    seq_group = owner.shape[1]
    length = target_ids.shape[0] // seq_group
    shards = lax.axis_size("vocab")
    own_count = seq_group // shards
    slots_row = owner[0]
    slot_index = lax.broadcasted_iota(jnp.int32, (seq_group, seq_group), 0)
    reorder = (slot_index == slots_row[None, :]).astype(jnp.float32)
    ordered_peak = jnp.dot(
        reorder, peak.reshape(seq_group, length), precision=lax.Precision.HIGHEST
    )
    ordered_sum = jnp.dot(
        reorder, expsum.reshape(seq_group, length), precision=lax.Precision.HIGHEST
    )
    ordered_pick = jnp.dot(
        reorder, picked.reshape(seq_group, length), precision=lax.Precision.HIGHEST
    )
    got_peak, got_sum, got_pick = side_by_side(
        (ordered_peak, ordered_sum, ordered_pick), "vocab", 0, 0, 1
    )
    got_peak = got_peak.reshape(shards, own_count, length)
    got_sum = got_sum.reshape(shards, own_count, length)
    got_pick = got_pick.reshape(shards, own_count, length)
    top = jnp.max(got_peak, axis=0)
    total = jnp.sum(got_sum * jnp.exp(got_peak - top[None]), axis=0)
    return top + jnp.log(total) - jnp.sum(got_pick, axis=0)


def solution(mesh):
    return jax.shard_map(
        local,
        mesh=mesh,
        in_specs=(P(("dp", "vocab"), None), P("dp"), P("dp", None), P(None, "vocab")),
        out_specs=P(("dp", "vocab"), None),
        check_vma=False,
    )
```

profile of v0, /device:TPU:0, one launch (start us, length us, event | category | flops | bytes accessed | tf_op | source)
XLA Modules:
  0.0 162.2 jit_solution(14684987293334065380)
XLA Ops:
  6.5 0.0 all-gather.2.cloned.1.call-start
  6.5 0.7 all-gather.2.cloned.1.call-update
  7.3 0.7 reshape.34
  8.0 50.4 %all-gather.2.cloned.1.call-done = bf16[1536,896]{1,0:T(8,128)(2,1)} async-done(((bf16[96,896]{1,0:T(8,128)(2,1)}), bf16[1536,896]{1,0:T(8,128)(2,1)}) %all-gather.2.cloned.1.call-update) | async-done | bytes 2752528 | tf_op jit(solution)/shard_map/all_gather | solution.py:36
  58.3 0.0 copy-start
  58.3 83.0 %while.10 = (s32[]{:T(128)}, f32[3,3,512]{2,1,0:T(4,128)S(1)}, bf16[3,512,896]{2,1,0:T(8,128)(2,1)}, bf16[896,9496]{0,1:T(8,128)(2,1)}, s32[3,512]{1,0:T(4,128)S(1)}, /*index=5*/s32[]{:T(128)}, s32[]{:T(128)}) while((s32[]{:T(128)}, f32[3,3,512]{2,1,0:T(4,128)S(1)}, bf16[3,512,896]{2,1,0:T(8,128)(2,1)}, bf16[896,9496]{0,1:T(8,128)(2,1)}, ...), condition=%wide.region_4.5_spmd, body=%wide.region_0.4_spmd.sunk | while | flops 8741791744 | bytes 56859224 | solution.py:41
  58.3 17.9 %fusion.21 = (f32[512]{0:T(512)S(1)}, f32[512,9496]{0,1:T(8,128)}) fusion(bf16[896,9496]{0,1:T(8,128)(2,1)} %get-tuple-element.122, bf16[3,512,896]{2,1,0:T(8,128)(2,1)} %get-tuple-element.121, s32[]{:T(128)} %get-tuple-element.112), kind=kOutput, calls=%fused_computation.23.clone.1 | convolution fusion | flops 8717479936 | bytes 37384704 | tf_op jit(solution)/shard_map/while/body/eval_jaxpr/dot_general | solution.py:29
  76.3 9.6 %exponential_reduce_fusion.2 = (f32[512]{0:T(512)S(1)}, f32[512]{0:T(512)S(1)}) fusion(f32[512,9496]{0,1:T(8,128)} %get-tuple-element.101, f32[512]{0:T(512)S(1)} %get-tuple-element.102, s32[512]{0:T(512)S(1)} %bitcast.34), kind=kLoop, calls=%fused_computation.2.clone.1 | loop fusion | flops 24308736 | bytes 19456000 | tf_op jit(solution)/shard_map/while/body/eval_jaxpr/reduce_sum | solution.py:31
  86.0 18.0 %fusion.21 = (f32[512]{0:T(512)S(1)}, f32[512,9496]{0,1:T(8,128)}) fusion(bf16[896,9496]{0,1:T(8,128)(2,1)} %get-tuple-element.122, bf16[3,512,896]{2,1,0:T(8,128)(2,1)} %get-tuple-element.121, s32[]{:T(128)} %get-tuple-element.112), kind=kOutput, calls=%fused_computation.23.clone.1 | convolution fusion | flops 8717479936 | bytes 37384704 | tf_op jit(solution)/shard_map/while/body/eval_jaxpr/dot_general | solution.py:29
  104.0 9.6 %exponential_reduce_fusion.2 = (f32[512]{0:T(512)S(1)}, f32[512]{0:T(512)S(1)}) fusion(f32[512,9496]{0,1:T(8,128)} %get-tuple-element.101, f32[512]{0:T(512)S(1)} %get-tuple-element.102, s32[512]{0:T(512)S(1)} %bitcast.34), kind=kLoop, calls=%fused_computation.2.clone.1 | loop fusion | flops 24308736 | bytes 19456000 | tf_op jit(solution)/shard_map/while/body/eval_jaxpr/reduce_sum | solution.py:31
  113.7 17.9 %fusion.21 = (f32[512]{0:T(512)S(1)}, f32[512,9496]{0,1:T(8,128)}) fusion(bf16[896,9496]{0,1:T(8,128)(2,1)} %get-tuple-element.122, bf16[3,512,896]{2,1,0:T(8,128)(2,1)} %get-tuple-element.121, s32[]{:T(128)} %get-tuple-element.112), kind=kOutput, calls=%fused_computation.23.clone.1 | convolution fusion | flops 8717479936 | bytes 37384704 | tf_op jit(solution)/shard_map/while/body/eval_jaxpr/dot_general | solution.py:29
  131.6 9.6 %exponential_reduce_fusion.2 = (f32[512]{0:T(512)S(1)}, f32[512]{0:T(512)S(1)}) fusion(f32[512,9496]{0,1:T(8,128)} %get-tuple-element.101, f32[512]{0:T(512)S(1)} %get-tuple-element.102, s32[512]{0:T(512)S(1)} %bitcast.34), kind=kLoop, calls=%fused_computation.2.clone.1 | loop fusion | flops 24308736 | bytes 19456000 | tf_op jit(solution)/shard_map/while/body/eval_jaxpr/reduce_sum | solution.py:31
  141.3 0.1 slice_reduce_fusion.2
  141.4 0.1 reshape_squeeze.11
  141.5 0.1 reshape_squeeze.10
  141.5 0.0 copy-done
  141.5 0.2 fusion.5
  141.7 0.2 fusion.6
  141.9 0.1 reshape_squeeze.9
  142.0 0.2 fusion.7
  142.3 0.1 copy.6
  142.4 12.1 %all_to_all.12 = f32[16,3,96]{2,1,0:T(4,128)S(1)} all-to-all(f32[16,3,96]{2,1,0:T(4,128)S(1)} %all_to_all.8), channel_id=1, replica_groups=mesh['dp'=8,'vocab'=16] {'vocab'}, dimensions={0} | all-to-all | bytes 36864 | tf_op jit(solution)/shard_map/all_to_all | solution.py:17
  154.5 0.1 fusion.12
  154.7 0.6 add_subtract_fusion
  (16 shorter events, 0.3 us)
Async XLA Ops:
  6.5 51.8 %all-gather.2.cloned.1.call-start = ((), (), s32[]{:S(2)}) async-start(), calls=%async_computation.1 | async-start | bytes 2924544 | tf_op jit(solution)/shard_map/all_gather | solution.py:36
  58.3 83.2 %copy-start = (s32[1,48]{1,0:T(1,128)S(1)}, s32[1,48]{1,0:T(1,128)}, u32[]{:S(2)}) copy-start(s32[1,48]{1,0:T(1,128)} %param.8) | copy-start | bytes 580
Sparse Core Ops, SparseCore 0:
  9.5 48.8 all-gather.1
where the time goes:
time: 163 us; the launch traced here: 162 us
  matrix products  54.5 us (33%)
  waiting for transfers between devices  51.1 us (31%)
  other arithmetic  29.7 us (18%)
  between operations  13.5 us (8%)
  blocking collectives  12.1 us (7%)
    dot_general x3, matrix products, partials(): logits = jnp.dot(rows, head, preferred_element_type=jnp.float32)  53.9 us
    all_gather x1, waiting for transfers between devices, local(): gathered = lax.all_gather(hidden, 'vocab', axis=0, tiled=True)  50.4 us
    reduce_sum x3, other arithmetic, partials(): expsum = jnp.sum(jnp.exp(logits - peak[:, None]), axis=1)  28.9 us
    all_to_all x1, blocking collectives, side_by_side(): lax.all_to_all(both, axis, split_axis=split_dim, concat_axis=concat_dim,...  12.1 us
  transfers between devices with their start and end apart: 1, of which 1 were waited for; matrix products, arithmetic and copies ran while one was open for 0% of the time, Pallas kernels for 0%

commit v1 on v0

v1 whole, which is shorter than its diff:
```python
import functools

import jax
import jax.numpy as jnp
from jax import lax
from jax.experimental import pallas as pl
from jax.experimental.pallas import tpu as pltpu
from jax.sharding import PartitionSpec as P

MESH = pl.DeviceIdType.MESH
SIDE = 4
PEERS = SIDE * SIDE
TILE = 256
PAIR = 2 * TILE
LOW = -1e30

OWN = [(0, 0, 0), (0, 0, 1)]
FIRST = [(1, 0, 0), (3, 0, 0), (0, 1, 1), (0, 3, 1)]
SECOND = [(2, 0, 0), (0, 2, 1)]
DIRECT = [(0, 1, 0), (0, 3, 0), (1, 0, 1), (3, 0, 1), (0, 2, 0), (2, 0, 1)]
RELAYED = [
    (dx, dy, half)
    for a, b in ((1, 1), (1, 3), (3, 1), (3, 3), (1, 2), (3, 2), (2, 1), (2, 3), (2, 2))
    for dx, dy, half in ((a, b, 0), (b, a, 1))
]
UNITS = OWN + FIRST + SECOND + DIRECT + RELAYED
SLOT = {unit: i for i, unit in enumerate(UNITS)}


def mult(value, of):
    return value if isinstance(value, int) else pl.multiple_of(value, of)


def kernel(
    hidden_ref, target_ref, owner_ref, head_ref, out_ref,
    xbuf, wbuf, wtail, wpad, tok, lab, peak_ref, sum_ref, pick_ref, flat, ordered, got,
    own_sem, head_sem, send_sem, recv_sem, out_sem, in_sem, entered,
):
    rows_own, depth = hidden_ref.shape
    width = head_ref.shape[1]
    half_rows = rows_own // 2
    count = xbuf.shape[0]
    block = 4 * half_rows
    groups = count // block
    pairs = wbuf.shape[1] // PAIR
    whole = width // PAIR
    edge = width // 128 * 128
    steps = groups * pairs

    me = lax.axis_index("vocab")
    y, x = lax.div(me, SIDE), lax.rem(me, SIDE)

    def at(dx, dy):
        return {"vocab": lax.rem(y + dy, SIDE) * SIDE + lax.rem(x + dx, SIDE)}

    own_copy = pltpu.make_async_copy(hidden_ref, xbuf.at[pl.ds(0, rows_own)], own_sem)
    own_copy.start()

    def head_chunk(i):
        cols = pl.ds(mult(i * PAIR, PAIR), PAIR)
        return pltpu.make_async_copy(head_ref.at[:, cols], wbuf.at[:, cols], head_sem.at[i])

    rest = pl.ds(whole * PAIR, edge - whole * PAIR)
    rest_copy = pltpu.make_async_copy(head_ref.at[:, rest], wbuf.at[:, rest], head_sem.at[whole])
    tail_copy = pltpu.make_async_copy(
        head_ref.at[:, pl.ds(edge, width - edge)], wtail, head_sem.at[whole + 1]
    )
    for i in range(whole):
        head_chunk(i).start()
    rest_copy.start()
    tail_copy.start()

    barrier = pltpu.get_barrier_semaphore()
    for d in (1, 2, 3):
        pl.semaphore_signal(barrier, inc=1, device_id=at(d, 0), device_id_type=MESH)
        pl.semaphore_signal(barrier, inc=1, device_id=at(0, d), device_id_type=MESH)
    pl.semaphore_wait(barrier, 6)

    sends = []

    def send(src, unit, dx, dy):
        there = ((unit[0] - dx) % SIDE, (unit[1] - dy) % SIDE, unit[2])
        slot = SLOT[there]
        copy = pltpu.make_async_remote_copy(
            src_ref=src,
            dst_ref=xbuf.at[pl.ds(slot * half_rows, half_rows)],
            send_sem=send_sem.at[len(sends)],
            recv_sem=recv_sem.at[slot],
            device_id=at(dx, dy),
            device_id_type=MESH,
        )
        copy.start()
        sends.append(unit)

    def arrived(slot):
        here = xbuf.at[pl.ds(mult(slot * half_rows, half_rows), half_rows)]
        pltpu.make_async_remote_copy(
            src_ref=here, dst_ref=here, send_sem=send_sem.at[0], recv_sem=recv_sem.at[slot],
            device_id=at(1, 0), device_id_type=MESH,
        ).wait_recv()

    def piece(unit):
        return xbuf.at[pl.ds(SLOT[unit] * half_rows, half_rows)]

    mine = [hidden_ref.at[pl.ds(h * half_rows, half_rows)] for h in (0, 1)]
    for d in (1, 3, 2):
        send(mine[0], OWN[0], d, 0)
        send(mine[1], OWN[1], 0, d)
    for d in (1, 3, 2):
        send(mine[0], OWN[0], 0, d)
        send(mine[1], OWN[1], d, 0)
    for d in (1, 2, 3):
        pl.semaphore_signal(entered, inc=1, device_id=at(0, d), device_id_type=MESH)

    lane = lax.broadcasted_iota(jnp.int32, (128, 128), 1)
    base = me * width
    for i in range(count // 128):
        ids = jnp.broadcast_to(target_ref[i : i + 1, :], (128, 128)).T - base
        tok[i * 128 : (i + 1) * 128, :] = (
            jnp.where((ids >= 0) & (ids < width), ids, -(1 << 24)) - lane
        )

    def place(unit):
        dx, dy, half = unit
        source = lax.rem(y + dy, SIDE) * SIDE + lax.rem(x + dx, SIDE)
        return mult(source * rows_own + half * half_rows, half_rows)

    for i, unit in enumerate(UNITS):
        lab[i * half_rows : (i + 1) * half_rows, :] = tok[pl.ds(place(unit), half_rows), :]
    peak_ref[...] = jnp.full_like(peak_ref, LOW)
    sum_ref[...] = jnp.zeros_like(sum_ref)
    pick_ref[...] = jnp.zeros_like(pick_ref)
    wpad[...] = jnp.zeros_like(wpad)
    ahead = whole * PAIR
    over = lax.broadcasted_iota(jnp.int32, (16, wbuf.shape[1] - ahead), 1) + ahead >= width
    top_row = lax.broadcasted_iota(jnp.int32, (16, wbuf.shape[1] - ahead), 0) == 0
    wpad[:, ahead:] = jnp.where(over & top_row, LOW, 0.0).astype(jnp.bfloat16)
    wbuf[:, edge:] = jnp.zeros((depth, wbuf.shape[1] - edge), jnp.bfloat16)

    own_copy.wait()
    for unit in FIRST:
        arrived(SLOT[unit])
        for d in (1, 3, 2):
            send(piece(unit), unit, *((0, d) if unit[2] == 0 else (d, 0)))

    def multiply(*accs):
        acc = [[accs[0], accs[1]], [accs[2], accs[3]]]
        last = depth // TILE
        left = depth - last * TILE
        ones = (lax.broadcasted_iota(jnp.int32, (block, TILE - left), 1) == 0).astype(jnp.float32)
        ones = ones.astype(jnp.bfloat16)

        def push(k, c, reg):
            for u in range(2):
                cols = pl.ds(mult(c + u * TILE, TILE), TILE)
                if k < last:
                    rhs = wbuf[k * TILE : (k + 1) * TILE, cols]
                else:
                    fill = jnp.zeros((TILE - left - 16, TILE), jnp.bfloat16)
                    rhs = jnp.concatenate([wbuf[k * TILE :, cols], wpad[:, cols], fill], axis=0)
                pltpu.matmul_push_rhs(rhs, reg, u)

        def where_is(n):
            g = n // pairs if isinstance(n, int) else lax.div(n, pairs)
            return mult(g * block, block), mult((n - g * pairs) * PAIR, PAIR)

        def mm(r, c, after, slot):
            for k in range(last + 1):
                if k < last:
                    push(k + 1, c, (k + 1) % 2)
                    lhs = xbuf[pl.ds(r, block), k * TILE : (k + 1) * TILE]
                else:
                    push(0, after, (k + 1) % 2)
                    lhs = jnp.concatenate([xbuf[pl.ds(r, block), k * TILE :], ones], axis=1)
                for u in range(2):
                    pltpu.matmul_acc_lhs(acc[u][slot], lhs, load_staged_rhs=k % 2)

        def statistics(r, c, slot):
            rows = pl.ds(r, block)
            a, b = pltpu.matmul_pop(acc[0][slot]), pltpu.matmul_pop(acc[1][slot])
            logits = [a[:, :128], a[:, 128:], b[:, :128], b[:, 128:]]
            label = lab[rows, :] - c
            old, total, picked = peak_ref[rows, :], sum_ref[rows, :], pick_ref[rows, :]
            peak = old
            for v in logits:
                peak = jnp.maximum(peak, v)
            total = total * jnp.exp(old - peak)
            for v in logits:
                total = total + jnp.exp(v - peak)
            for i, v in enumerate(logits):
                picked = jnp.where(label == i * 128, v, picked)
            peak_ref[rows, :], sum_ref[rows, :], pick_ref[rows, :] = peak, total, picked

        head_chunk(0).wait()
        head_chunk(1).wait()
        push(0, 0, 0)
        mm(*where_is(0), PAIR, 0)

        def arrivals(q, g, lo, hi):
            first = (g * pairs - 1) // 2

            @pl.when(q == first)
            def _():
                if g == 1:
                    for unit in SECOND:
                        arrived(SLOT[unit])
                        for d in (1, 3, 2):
                            send(piece(unit), unit, *((0, d) if unit[2] == 0 else (d, 0)))
                else:

                    @pl.loop(lo, hi)
                    def _(slot):
                        arrived(slot)

        @pl.loop(0, (steps - 2) // 2)
        def _(q):
            @pl.when(q < (whole - 2) // 2)
            def _():
                head_chunk(2 * q + 2).wait()
                head_chunk(2 * q + 3).wait()

            @pl.when(q == (whole - 2) // 2)
            def _():
                rest_copy.wait()
                tail_copy.wait()
                wbuf[:, edge : edge + 128] = jnp.concatenate(
                    [wtail[...], jnp.zeros((depth, 128 - (width - edge)), jnp.bfloat16)], axis=1
                )

            for g in range(1, groups):
                arrivals(q, g, g * 4, g * 4 + 4)
            spots = [where_is(2 * q + j) for j in range(4)]
            for j in range(2):
                mm(*spots[j + 1], spots[j + 2][1], (j + 1) % 2)
                statistics(*spots[j], j % 2)

        before, final = where_is(steps - 2), where_is(steps - 1)
        mm(*final, 0, 1)
        statistics(*before, 0)
        for u in range(2):
            pltpu.matmul_acc_lhs(acc[u][0], jnp.zeros((block, TILE), jnp.bfloat16), load_staged_rhs=0)
        statistics(*final, 1)
        for u in range(2):
            pltpu.matmul_pop(acc[u][0])

    pl.run_scoped(multiply, *[pltpu.ACC(u)((block, TILE), jnp.float32) for u in (0, 0, 1, 1)])

    seq_count = owner_ref.shape[1]
    length = count // seq_count
    lanes = lax.broadcasted_iota(jnp.int32, (half_rows, 128), 1)
    for i, unit in enumerate(UNITS):
        rows = slice(i * half_rows, (i + 1) * half_rows)
        peak = jnp.max(peak_ref[rows, :], axis=1, keepdims=True)
        total = jnp.sum(sum_ref[rows, :] * jnp.exp(peak_ref[rows, :] - peak), axis=1, keepdims=True)
        picked = jnp.sum(pick_ref[rows, :], axis=1, keepdims=True)
        flat[pl.ds(place(unit), half_rows), :] = jnp.where(
            lanes < length, peak, jnp.where(lanes < 2 * length, total, picked)
        )
    spot = lax.broadcasted_iota(jnp.int32, (count, 128), 0) % length
    lanes = lax.broadcasted_iota(jnp.int32, (count, 128), 1)
    by_token = jnp.where((lanes % length == spot) & (lanes < 3 * length), flat[...], 0.0)
    by_seq = jnp.sum(by_token.reshape(seq_count, length, 128), axis=1)
    owned = seq_count // PEERS
    row = lax.broadcasted_iota(jnp.int32, (8 * PEERS, 128), 0)
    slot_of = jnp.where(row % 8 < owned, row // 8 * owned + row % 8, -1)
    sorted_rows = jnp.zeros((8 * PEERS, 128), jnp.float32)
    for i in range(seq_count):
        owner = jnp.broadcast_to(owner_ref[:, i : i + 1], (1, 128))
        sorted_rows = jnp.where(slot_of == owner, by_seq[i : i + 1, :], sorted_rows)
    ordered[...] = sorted_rows

    pl.semaphore_wait(entered, 3)
    outs = []
    for d in range(1, PEERS):
        to = lax.rem(me + d, PEERS)
        copy = pltpu.make_async_remote_copy(
            src_ref=ordered.at[pl.ds(mult(to * 8, 8), 8)],
            dst_ref=got.at[d],
            send_sem=out_sem.at[d],
            recv_sem=in_sem.at[d],
            device_id={"vocab": to},
            device_id_type=MESH,
        )
        copy.start()
        outs.append(copy)
    got[0] = ordered[pl.ds(mult(me * 8, 8), 8), :]
    for copy in outs:
        copy.wait_recv()
    top = got[0]
    for d in range(1, PEERS):
        top = jnp.maximum(top, got[d])
    total, picked = jnp.zeros_like(top), jnp.zeros_like(top)
    for d in range(PEERS):
        scale = pltpu.roll(jnp.exp(got[d] - top), length, 1)
        total = total + got[d] * scale
        picked = picked + got[d]
    loss = top[:, :length] + jnp.log(total[:, length : 2 * length]) - picked[:, 2 * length : 3 * length]
    out_ref[...] = loss[:owned, :]
    for i, unit in enumerate(sends):
        pltpu.make_async_remote_copy(
            src_ref=piece(unit), dst_ref=piece(unit), send_sem=send_sem.at[i], recv_sem=recv_sem.at[0],
            device_id=at(1, 0), device_id_type=MESH,
        ).wait_send()
    for copy in outs:
        copy.wait_send()


def local(hidden, target_ids, owner, head):
    rows_own, depth = hidden.shape
    count = target_ids.shape[0]
    width = head.shape[1]
    wide = -(-width // PAIR) * PAIR
    seq_count = owner.shape[1]
    length = count // seq_count
    vmem = pl.BlockSpec(memory_space=pltpu.VMEM)
    anywhere = pl.BlockSpec(memory_space=pl.ANY)
    stat = pltpu.VMEM((count, 128), jnp.float32)
    return pl.pallas_call(
        kernel,
        out_shape=jax.ShapeDtypeStruct((seq_count // PEERS, length), jnp.float32),
        in_specs=[anywhere, vmem, vmem, anywhere],
        out_specs=vmem,
        scratch_shapes=[
            pltpu.VMEM((count, depth), jnp.bfloat16),
            pltpu.VMEM((depth, wide), jnp.bfloat16),
            pltpu.VMEM((depth, width % 128), jnp.bfloat16),
            pltpu.VMEM((16, wide), jnp.bfloat16),
            pltpu.VMEM((count, 128), jnp.int32),
            pltpu.VMEM((count, 128), jnp.int32),
            stat, stat, stat, stat,
            pltpu.VMEM((8 * PEERS, 128), jnp.float32),
            pltpu.VMEM((PEERS, 8, 128), jnp.float32),
            pltpu.SemaphoreType.DMA,
            pltpu.SemaphoreType.DMA((width // PAIR + 2,)),
            pltpu.SemaphoreType.DMA((len(UNITS),)),
            pltpu.SemaphoreType.DMA((len(UNITS),)),
            pltpu.SemaphoreType.DMA((PEERS,)),
            pltpu.SemaphoreType.DMA((PEERS,)),
            pltpu.SemaphoreType.REGULAR,
        ],
        compiler_params=pltpu.CompilerParams(collective_id=0, has_side_effects=True),
    )(hidden, target_ids.reshape(count // 128, 128), owner, head)


def solution(mesh):
    return jax.shard_map(
        local,
        mesh=mesh,
        in_specs=(P(("dp", "vocab"), None), P("dp"), P("dp", None), P(None, "vocab")),
        out_specs=P(("dp", "vocab"), None),
        check_vma=False,
    )
```

time: 163 us -> 89.5 us (0.55)
  Pallas kernels: 0 us -> 65 us
  matrix products: 54.5 us -> 0 us
  waiting for transfers between devices: 51.1 us -> 0 us
  other arithmetic: 29.7 us -> 0 us
  local copies, waits for them, and re-layouts: 1.24 us -> 23.8 us
  between operations: 13.5 us -> 0.01 us
  blocking collectives: 12.1 us -> 0 us
    pallas_call x0 -> x1, Pallas kernels: none -> 65 us  [local(): pl.pallas_call(kernel, out_shape=jax.ShapeDtypeStruct((seq_count // PEERS...]
    dot_general x6 -> x0, matrix products: 54.5 us -> none  [the longest x3 53.9 us: partials(): logits = jnp.dot(rows, head, preferred_element_type=jnp.float32)]
    all_gather x1 -> x0, waiting for transfers between devices: 50.4 us -> none  [local(): gathered = lax.all_gather(hidden, 'vocab', axis=0, tiled=True)]
    reduce_sum x5 -> x0, other arithmetic: 29 us -> none  [the longest x3 28.9 us: partials(): expsum = jnp.sum(jnp.exp(logits - peak[:, None]), axis=1)]
    unnamed x2, local copies, waits for them, and re-layouts: 0.01 us -> 23.8 us
    all_to_all x1 -> x0, blocking collectives: 12.1 us -> none  [side_by_side(): lax.all_to_all(both, axis, split_axis=split_dim, concat_axis=concat_dim,...]
  transfers between devices with their start and end apart: 1 -> 0, of which waited for: 1 -> 0; matrix products, arithmetic and copies ran while one was open for 0% -> 0% of each run, Pallas kernels for 0% -> 0%
where the time goes in v1:
time: 89.5 us; the launch traced here: 88.8 us
  Pallas kernels  65 us (73%)
  local copies, waits for them, and re-layouts  23.8 us (27%)
    pallas_call x1, Pallas kernels, local(): pl.pallas_call(kernel, out_shape=jax.ShapeDtypeStruct((seq_count // PEERS...  65 us
    unnamed x2, local copies, waits for them, and re-layouts  23.8 us

profile of v1, /device:TPU:0, one launch (start us, length us, event | category | flops | bytes accessed | tf_op | source)
XLA Modules:
  0.0 88.8 jit_solution(2105739544242586598)
XLA Ops:
  0.0 22.6 %copy.5.head_ref = bf16[896,9496]{1,0:T(8,128)(2,1)} copy(bf16[896,9496]{0,1:T(8,128)(2,1)} %param.7) | data formatting | bytes 34033664 | tf_op args[3]
  22.6 65.0 %shard_map.46 = f32[3,32]{1,0:T(4,128)} custom-call(bf16[96,896]{1,0:T(8,128)(2,1)} %hidden_ref.1, s32[12,128]{1,0:T(8,128)} %bitcast.1, s32[1,48]{1,0:T(1,128)} %owner_ref.1, bf16[896,9496]{1,0:T(8,128)(2,1)} %copy.5.head_ref), custom_call_target="tpu_custom_call" | custom-call | tf_op jit(solution)/shard_map/pallas_call | solution.py:318
  87.5 1.2 %copy.7 = f32[3,32]{1,0:T(4,128)} copy(f32[3,32]{1,0:T(4,128)} %shard_map.46) | data formatting | bytes 768
